TPU v7x, 32 devices: a whole 2x2x4 slice. The times are simulated.
32 devices in a mesh: dom: 8 (over z, y), sub: 4 (over x, core).
Axes of the slice: x: 2, y: 2, z: 4, core: 2. Of those that a mesh axis runs over, the one named last changes fastest.
Arguments:
- nodes: bfloat16 [16384, 128], P(('dom', 'sub')), may hold values from -6 to 6
- edges: bfloat16 [65536, 128], P(('dom', 'sub')), may hold values from -6 to 6
- senders: int32 [65536], P(('dom', 'sub')), may hold values from 0 to 895
- receivers: int32 [65536], P(('dom', 'sub')), may hold values from 0 to 511
- edge_live: int32 [65536], P(('dom', 'sub')), may hold values from 0 to 1, as said below
- outlet_flags: int32 [16384], P(('dom', 'sub')), may hold values 0 or 1
- send_rows: int32 [12288], P(('dom', 'sub')), may hold values from 0 to 511
- edge_first: float32 [3, 384, 128], replicated, may hold values from -0.3125 to 0.3125
- edge_bias: float32 [3, 128], replicated, may hold values from -3 to 3
- edge_second: float32 [3, 128, 128], replicated, may hold values from -0.5 to 0.5
- edge_offset: float32 [3, 128], replicated, may hold values from -3 to 3
- edge_gain: float32 [3, 128], replicated, may hold values from 0.25 to 1.75
- node_first: float32 [3, 256, 128], replicated, may hold values from -0.375 to 0.375
- node_bias: float32 [3, 128], replicated, may hold values from -3 to 3
- node_second: float32 [3, 128, 128], replicated, may hold values from -0.5 to 0.5
- node_offset: float32 [3, 128], replicated, may hold values from -3 to 3
- node_gain: float32 [3, 128], replicated, may hold values from 0.25 to 1.75
- outlet_map: float32 [3, 128, 128], replicated, may hold values from -0.5 to 0.5
- grad_out: float32 [16384, 128], P(('dom', 'sub')), may hold values from -6 to 6
Outputs:
- latent_out: float32 [16384, 128], P(('dom', 'sub'))
- latent_grad: float32 [16384, 128], P(('dom', 'sub'))
- edge_first_grad: float32 [3, 384, 128], replicated
- edge_bias_grad: float32 [3, 128], replicated
- edge_second_grad: float32 [3, 128, 128], replicated
- edge_offset_grad: float32 [3, 128], replicated
- edge_gain_grad: float32 [3, 128], replicated
- node_first_grad: float32 [3, 256, 128], replicated
- node_bias_grad: float32 [3, 128], replicated
- node_second_grad: float32 [3, 128, 128], replicated
- node_offset_grad: float32 [3, 128], replicated
- node_gain_grad: float32 [3, 128], replicated
- outlet_map_grad: float32 [3, 128, 128], replicated
Inputs may be any that keep to these rules, and one draw needn't show every extreme that they name: `edge_live`: on each device the live edge slots are the first ones of its 2048; each device has between a quarter and all of them live, and some device has all live. `senders`: indices below 512 name the device's own nodes; higher ones name halo rows.
All inputs are finite; a program needn't handle non-finite values. No bound on the sum of `outlet_flags` on one device may be relied on, other than what follows from the above.
Results may differ from a plain program's by a relative error of at most 0.018.
Values may be sent and summed in bfloat16 or wider, within the bound.
A program may use at most 320 MiB of HBM per device.

v0:
```python
import jax
import jax.numpy as jnp
from jax import lax
from jax.sharding import PartitionSpec as P


def passed_along(value, axis, steps):
    count = lax.axis_size(axis)
    first, last = (max(0, -steps), min(count, count - steps))
    return lax.ppermute(value, axis, [(source, source + steps) for source in range(first, last)])


def normalize(values):
    mean = jnp.mean(values, axis=-1, keepdims=True)
    centered = values - mean
    variance = jnp.mean(centered * centered, axis=-1, keepdims=True)
    return centered * lax.rsqrt(variance + 1e-05)


def layer_local(latent, edge_state, halo, layer_weights, senders, receivers, live, flags):
    (
        edge_first,
        edge_bias,
        edge_second,
        edge_offset,
        edge_gain,
        node_first,
        node_bias,
        node_second,
        node_offset,
        node_gain,
        outlet_map,
    ) = layer_weights
    own = latent.astype(jnp.bfloat16)
    extended = jnp.concatenate([own, halo], axis=0)
    joined = jnp.concatenate(
        [edge_state.astype(jnp.bfloat16), extended[senders], own[receivers]], axis=1
    )
    act_one = jax.nn.silu(
        jnp.dot(joined, edge_first.astype(jnp.bfloat16), preferred_element_type=jnp.float32)
        + edge_bias
    ).astype(jnp.bfloat16)
    pre_two = (
        jnp.dot(act_one, edge_second.astype(jnp.bfloat16), preferred_element_type=jnp.float32)
        + edge_offset
    )
    message = live[:, None] * (edge_gain * normalize(pre_two))
    new_edge = edge_state + message
    summed = jax.ops.segment_sum(message, receivers, num_segments=latent.shape[0])
    summed_half = summed.astype(jnp.bfloat16)
    node_in = jnp.concatenate([own, summed_half], axis=1)
    node_hidden = jax.nn.silu(
        jnp.dot(node_in, node_first.astype(jnp.bfloat16), preferred_element_type=jnp.float32)
        + node_bias
    ).astype(jnp.bfloat16)
    update = node_gain * normalize(
        jnp.dot(node_hidden, node_second.astype(jnp.bfloat16), preferred_element_type=jnp.float32)
        + node_offset
    )
    outlet = flags[:, None] * jnp.dot(
        summed_half, outlet_map.astype(jnp.bfloat16), preferred_element_type=jnp.float32
    )
    return (latent + update + outlet, new_edge)


def send_halo(latent, send_rows, low, high):
    sent = latent[send_rows].astype(jnp.bfloat16)
    from_lower = passed_along(sent[low : 2 * low], "sub", 1)
    from_upper = passed_along(sent[:low], "sub", -1)
    dom_lower = passed_along(sent[2 * low + high :], "dom", 1)
    dom_upper = passed_along(sent[2 * low : 2 * low + high], "dom", -1)
    return jnp.concatenate([from_lower, from_upper, dom_lower, dom_upper], axis=0)


def return_halo(halo_grad, send_rows, low, high, shape):
    back_high = passed_along(halo_grad[:low], "sub", -1)
    back_low = passed_along(halo_grad[low : 2 * low], "sub", 1)
    dom_back_high = passed_along(halo_grad[2 * low : 2 * low + high], "dom", -1)
    dom_back_low = passed_along(halo_grad[2 * low + high :], "dom", 1)
    returned = jnp.concatenate([back_low, back_high, dom_back_low, dom_back_high], axis=0).astype(
        jnp.float32
    )
    return jnp.zeros(shape, jnp.float32).at[send_rows].add(returned)


def flatten_all(grads):
    return jnp.concatenate([grad.reshape(-1) for grad in grads])


def unflatten_all(flat, shapes):
    pieces = []
    offset = 0
    for shape in shapes:
        length = 1
        for extent in shape:
            length = length * extent
        pieces.append(flat[offset : offset + length].reshape(shape))
        offset = offset + length
    return pieces


def on_device(
    nodes,
    edges,
    senders,
    receivers,
    edge_live,
    outlet_flags,
    send_rows,
    edge_first,
    edge_bias,
    edge_second,
    edge_offset,
    edge_gain,
    node_first,
    node_bias,
    node_second,
    node_offset,
    node_gain,
    outlet_map,
    grad_out,
):
    weights = (
        edge_first,
        edge_bias,
        edge_second,
        edge_offset,
        edge_gain,
        node_first,
        node_bias,
        node_second,
        node_offset,
        node_gain,
        outlet_map,
    )
    layers = edge_first.shape[0]
    low = nodes.shape[0] // 8
    high = nodes.shape[0] // 4
    live = edge_live.astype(jnp.float32)
    flags = outlet_flags.astype(jnp.float32)
    latent = nodes.astype(jnp.float32)
    edge_state = edges.astype(jnp.float32)

    def advance(latent_in, edge_in, halo, layer_weights):
        return layer_local(latent_in, edge_in, halo, layer_weights, senders, receivers, live, flags)

    saved = []
    for layer in range(layers):
        layer_weights = tuple((weight[layer] for weight in weights))
        halo = send_halo(latent, send_rows, low, high)
        (latent, edge_state), pullback = jax.vjp(advance, latent, edge_state, halo, layer_weights)
        saved.append(pullback)
    layer_shapes = [weight.shape[1:] for weight in weights]
    latent_grad = grad_out
    edge_grad = jnp.zeros_like(edge_state)
    per_layer = [None] * layers
    for layer in reversed(range(layers)):
        pullback = saved[layer]
        latent_grad, edge_grad, halo_grad, weight_grads = pullback((latent_grad, edge_grad))
        latent_grad = latent_grad + return_halo(halo_grad, send_rows, low, high, latent_grad.shape)
        flat = flatten_all(weight_grads)
        per_layer[layer] = flat
    stacked = jnp.stack(per_layer, axis=0)
    stacked = lax.psum(stacked, ("dom", "sub"))
    by_layer = [unflatten_all(stacked[layer], layer_shapes) for layer in range(layers)]
    results = [
        jnp.stack([by_layer[layer][which] for layer in range(layers)], axis=0)
        for which in range(len(weights))
    ]
    return (
        latent,
        latent_grad,
        results[0],
        results[1],
        results[2],
        results[3],
        results[4],
        results[5],
        results[6],
        results[7],
        results[8],
        results[9],
        results[10],
    )


def solution(mesh):
    placed = (
        P(("dom", "sub"), None),
        P(("dom", "sub"), None),
        P(("dom", "sub")),
        P(("dom", "sub")),
        P(("dom", "sub")),
        P(("dom", "sub")),
        P(("dom", "sub")),
        P(),
        P(),
        P(),
        P(),
        P(),
        P(),
        P(),
        P(),
        P(),
        P(),
        P(),
        P(("dom", "sub"), None),
    )
    return jax.shard_map(
        on_device,
        mesh=mesh,
        in_specs=placed,
        out_specs=(
            P(("dom", "sub"), None),
            P(("dom", "sub"), None),
            P(),
            P(),
            P(),
            P(),
            P(),
            P(),
            P(),
            P(),
            P(),
            P(),
            P(),
        ),
        check_vma=False,
    )
```

profile of v0, /device:TPU:1, one launch (start us, length us, event | category | flops | bytes accessed | tf_op | source)
XLA Modules:
  0.0 547.7 jit_solution(7893833300528265434)
XLA Ops:
  13.3 4.6 collective-permute-start
  19.9 4.6 collective-permute-start.2
  33.5 6.2 %gather_fusion.2 = bf16[2048,128]{1,0:T(8,128)(2,1)S(1)} fusion(bf16[512,128]{1,0:T(8,128)(2,1)S(1)} %copy-done, s32[2048]{0:T(1024)S(1)} %get-tuple-element.118), kind=kCustom, calls=%fused_computation.2 | custom fusion | bytes 1056768 | tf_op jit(solution)/shard_map/jvp()/gather | solution.py:37
  42.0 6.2 %gather_fusion.1 = bf16[2048,128]{1,0:T(8,128)(2,1)S(1)} fusion(bf16[896,128]{1,0:T(8,128)(2,1)S(1)} %constant_dynamic-update-slice_fusion, s32[2048]{0:T(1024)S(1)} %get-tuple-element.121), kind=kCustom, calls=%fused_computation.1 | custom fusion | bytes 1056768 | tf_op jit(solution)/shard_map/jvp()/gather | solution.py:37
  53.7 11.9 %scatter_custom_fusion = f32[512,128]{1,0:T(8,128)S(1)} fusion(s32[2048]{0:T(1024)S(1)} %copy-done.84, f32[2048,128]{1,0:T(8,128)} %copy.74, f32[]{:T(128)} %constant.51.clone.1), kind=kCustom, calls=%fused_computation.256 | custom fusion | flops 262144 | bytes 262656 | tf_op jit(solution)/shard_map/jvp()/scatter-add | solution.py:49
  71.2 4.7 collective-permute-start.6
  76.5 2.7 collective-permute-start.5
  79.2 3.4 collective-permute-start.4
  82.8 6.2 %gather_fusion.5 = bf16[2048,128]{1,0:T(8,128)(2,1)S(1)} fusion(bf16[512,128]{1,0:T(8,128)(2,1)S(1)} %copy.80, s32[2048]{0:T(1024)S(1)} %copy-done.66), kind=kCustom, calls=%fused_computation.5 | custom fusion | bytes 1056768 | tf_op jit(solution)/shard_map/jvp()/gather | solution.py:37
  91.8 6.2 %gather_fusion.4 = bf16[2048,128]{1,0:T(8,128)(2,1)S(1)} fusion(bf16[896,128]{1,0:T(8,128)(2,1)S(1)} %copy.79, s32[2048]{0:T(1024)S(1)} %copy-done.60), kind=kCustom, calls=%fused_computation.4 | custom fusion | bytes 1056768 | tf_op jit(solution)/shard_map/jvp()/gather | solution.py:37
  104.8 2.6 copy.83
  107.4 11.9 %scatter_custom_fusion.1 = f32[512,128]{1,0:T(8,128)S(1)} fusion(s32[2048]{0:T(1024)S(1)} %copy-done.85, f32[2048,128]{1,0:T(8,128)} %copy.83, f32[]{:T(128)} %constant.51.clone.1), kind=kCustom, calls=%fused_computation.254 | custom fusion | flops 262144 | bytes 262656 | tf_op jit(solution)/shard_map/jvp()/scatter-add | solution.py:49
  127.9 3.6 collective-permute-start.8
  132.8 5.0 collective-permute-start.10
  138.1 7.2 %gather_fusion.8 = bf16[2048,128]{1,0:T(8,128)(2,1)S(1)} fusion(bf16[512,128]{1,0:T(8,128)(2,1)S(1)} %copy.89, s32[2048]{0:T(1024)} %copy-done.65), kind=kCustom, calls=%fused_computation.8 | custom fusion | bytes 1056768 | tf_op jit(solution)/shard_map/jvp()/gather | solution.py:37
  147.4 7.2 %gather_fusion.7 = bf16[2048,128]{1,0:T(8,128)(2,1)S(1)} fusion(bf16[896,128]{1,0:T(8,128)(2,1)S(1)} %copy.88, s32[2048]{0:T(1024)} %copy-done.59), kind=kCustom, calls=%fused_computation.7 | custom fusion | bytes 1056768 | tf_op jit(solution)/shard_map/jvp()/gather | solution.py:37
  161.5 2.5 copy.92
  164.0 12.9 %scatter_custom_fusion.2 = f32[512,128]{1,0:T(8,128)} fusion(s32[2048]{0:T(1024)} %param.22, f32[2048,128]{1,0:T(8,128)} %copy.92, f32[]{:T(128)} %constant.51.clone.1), kind=kCustom, calls=%fused_computation.252 | custom fusion | flops 262144 | bytes 262656 | tf_op jit(solution)/shard_map/jvp()/scatter-add | solution.py:49
  190.3 8.4 %gather_fusion.9 = f32[2048,128]{1,0:T(8,128)} fusion(f32[512,128]{1,0:T(8,128)S(1)} %fusion.19, s32[2048]{0:T(1024)} %get-tuple-element.119), kind=kCustom, calls=%fused_computation.9 | custom fusion | bytes 2105344 | tf_op jit(solution)/shard_map/transpose(jvp())/gather | solution.py:49
  198.7 2.6 copy.97
  201.3 2.2 multiply_reduce_fusion
  212.9 11.9 %scatter_custom_fusion.3 = bf16[896,128]{1,0:T(8,128)(2,1)S(1)} fusion(s32[2048]{0:T(1024)} %get-tuple-element.120, bf16[2048,128]{1,0:T(8,128)(2,1)} %copy.99, bf16[]{:T(256)} %constant.59.clone.1), kind=kCustom, calls=%fused_computation.261 | custom fusion | flops 262144 | bytes 229888 | tf_op jit(solution)/shard_map/transpose(jvp())/scatter-add | solution.py:37
  227.3 2.2 collective-permute-start.12
  229.5 2.7 collective-permute-start.13
  232.2 4.3 collective-permute-start.14
  237.8 11.9 %scatter_fusion = bf16[512,128]{1,0:T(8,128)(2,1)S(1)} fusion(bf16[512,128]{1,0:T(8,128)(2,1)S(1)} %slice_add_fusion.2, s32[2048]{0:T(1024)} %get-tuple-element.117, bf16[2048,128]{1,0:T(8,128)(2,1)S(1)} %copy.100), kind=kCustom, calls=%fused_computation.16 | custom fusion | flops 262144 | bytes 1581056 | tf_op jit(solution)/shard_map/transpose(jvp())/scatter-add | solution.py:37
  264.7 3.6 stack.26
  268.3 3.2 scatter_custom_fusion.5
  280.3 7.6 %gather_fusion.10 = f32[2048,128]{1,0:T(8,128)} fusion(f32[512,128]{1,0:T(8,128)S(1)} %fusion.21, s32[2048]{0:T(1024)S(1)} %copy-done.70), kind=kCustom, calls=%fused_computation.10 | custom fusion | bytes 2105344 | tf_op jit(solution)/shard_map/transpose(jvp())/gather | solution.py:49
  301.8 11.9 %scatter_custom_fusion.6 = bf16[896,128]{1,0:T(8,128)(2,1)S(1)} fusion(s32[2048]{0:T(1024)} %get-tuple-element.120, bf16[2048,128]{1,0:T(8,128)(2,1)} %copy.105, bf16[]{:T(256)} %constant.59.clone.1), kind=kCustom, calls=%fused_computation.259 | custom fusion | flops 262144 | bytes 229888 | tf_op jit(solution)/shard_map/transpose(jvp())/scatter-add | solution.py:37
  316.3 11.8 %scatter_fusion.1 = bf16[512,128]{1,0:T(8,128)(2,1)S(1)} fusion(bf16[512,128]{1,0:T(8,128)(2,1)S(1)} %slice_add_fusion.1, s32[2048]{0:T(1024)} %get-tuple-element.117, bf16[2048,128]{1,0:T(8,128)(2,1)S(1)} %copy.106), kind=kCustom, calls=%fused_computation.19 | custom fusion | flops 262144 | bytes 1581056 | tf_op jit(solution)/shard_map/transpose(jvp())/scatter-add | solution.py:37
  329.1 3.4 collective-permute-start.16
  334.5 4.3 collective-permute-start.18
  354.3 3.6 stack.25
  357.9 2.9 scatter_custom_fusion.8
  370.2 8.4 %gather_fusion.11 = f32[2048,128]{1,0:T(8,128)} fusion(f32[512,128]{1,0:T(8,128)S(1)} %fusion.23, s32[2048]{0:T(1024)} %get-tuple-element.119), kind=kCustom, calls=%fused_computation.11 | custom fusion | bytes 2105344 | tf_op jit(solution)/shard_map/transpose(jvp())/gather | solution.py:49
  378.5 2.6 copy.109
  388.8 2.5 stack.24
  391.3 2.4 pad_maximum_fusion
  393.8 11.9 %scatter_custom_fusion.9 = bf16[896,128]{1,0:T(8,128)(2,1)S(1)} fusion(s32[2048]{0:T(1024)} %get-tuple-element.120, bf16[2048,384]{1,0:T(8,128)(2,1)S(1)} %convolution_convert_fusion, bf16[]{:T(256)} %constant.59.clone.1), kind=kCustom, calls=%fused_computation.171 | custom fusion | flops 262144 | bytes 754176 | tf_op jit(solution)/shard_map/transpose(jvp())/scatter-add | solution.py:37
  405.7 12.0 %scatter_custom_fusion.10 = bf16[512,128]{1,0:T(8,128)(2,1)S(1)} fusion(bf16[512,128]{1,0:T(8,128)(2,1)S(1)} %slice_add_fusion, s32[2048]{0:T(1024)} %get-tuple-element.117, bf16[2048,384]{1,0:T(8,128)(2,1)S(1)} %convolution_convert_fusion), kind=kCustom, calls=%fused_computation.169 | custom fusion | flops 262144 | bytes 655360 | tf_op jit(solution)/shard_map/transpose(jvp())/scatter-add | solution.py:37
  417.7 3.9 collective-permute-start.20
  423.6 4.3 collective-permute-start.22
  429.2 3.3 collective-permute-done.23
  432.5 2.9 scatter_custom_fusion.11
  435.4 94.2 %all-reduce.2.cloned.1.call-done = f32[3,131840]{1,0:T(4,128)} async-done(((f32[3,131840]{1,0:T(4,128)}), f32[3,131840]{1,0:T(4,128)}) %all-reduce.2.cloned.1.call-update) | async-done | bytes 1582096 | tf_op jit(solution)/shard_map/psum | solution.py:164
  532.1 2.3 fusion.165
  535.1 2.4 fusion.168
  (507 shorter events, 170.0 us)
Async XLA Ops:
  7.2 22.1 %copy-start = (bf16[512,128]{1,0:T(8,128)(2,1)S(1)}, bf16[512,128]{1,0:T(8,128)(2,1)}, u32[]{:S(2)}) copy-start(bf16[512,128]{1,0:T(8,128)(2,1)} %param.19) | copy-start | bytes 393220
  7.3 20.7 %copy-start.95 = (s32[2048]{0:T(1024)S(1)}, s32[2048]{0:T(1024)}, u32[]{:S(2)}) copy-start(s32[2048]{0:T(1024)} %param.21) | copy-start | bytes 24580
  7.3 21.3 %copy-start.84 = (s32[2048]{0:T(1024)S(1)}, s32[2048]{0:T(1024)}, u32[]{:S(2)}) copy-start(s32[2048]{0:T(1024)} %param.22) | copy-start | bytes 24580
  7.3 21.9 %copy-start.18 = (bf16[2048,128]{1,0:T(8,128)(2,1)S(1)}, bf16[2048,128]{1,0:T(8,128)(2,1)}, u32[]{:S(2)}) copy-start(bf16[2048,128]{1,0:T(8,128)(2,1)} %param.20) | copy-start | bytes 1572868
  7.3 522.3 %all-reduce.2.cloned.1.call-start = ((), (), s32[]{:S(2)}) async-start(), calls=%async_computation | async-start | bytes 4218880 | tf_op jit(solution)/shard_map/psum | solution.py:164
  8.1 22.1 %copy-start.96 = (s32[384]{0:T(512)}, s32[384]{0:T(512)S(1)}, u32[]{:S(2)}) copy-start(s32[384]{0:T(512)S(1)} %compare_select_fusion.2) | copy-start | bytes 4612
  9.3 21.0 %copy-start.104 = (s32[512]{0:T(512)S(1)}, s32[512]{0:T(512)}, u32[]{:S(2)}) copy-start(s32[512]{0:T(512)} %param.24) | copy-start | bytes 6148
  9.3 21.0 %copy-start.97 = (s32[2048]{0:T(1024)S(1)}, s32[2048]{0:T(1024)}, u32[]{:S(2)}) copy-start(s32[2048]{0:T(1024)} %param.23) | copy-start | bytes 24580
  9.3 21.0 %copy-start.56 = (f32[3,128,128]{2,1,0:T(8,128)S(1)}, f32[3,128,128]{2,1,0:T(8,128)}, u32[]{:S(2)}) copy-start(f32[3,128,128]{2,1,0:T(8,128)} %param.28) | copy-start | bytes 589828
  10.8 20.2 %copy-start.57 = (f32[3,128,128]{2,1,0:T(8,128)S(1)}, f32[3,128,128]{2,1,0:T(8,128)}, u32[]{:S(2)}) copy-start(f32[3,128,128]{2,1,0:T(8,128)} %param.33) | copy-start | bytes 589828
  11.4 29.1 %collective-permute-start.1 = (bf16[64,128]{1,0:T(8,128)(2,1)}, bf16[64,128]{1,0:T(8,128)(2,1)}, u32[]{:S(2)}, u32[]{:S(2)}) collective-permute-start(bf16[64,128]{1,0:T(8,128)(2,1)} %get-tuple-element.115), channel_id=1, source_target_pairs={{1,0},{2,1},{3,2},{5,4},{6,5},{7,6},{9,8},{10,9},{11,10},{13,12},{... | collective-permute-start | bytes 49160 | tf_op jit(solution)/shard_map/ppermute | solution.py:10
  13.3 26.4 %collective-permute-start = (bf16[64,128]{1,0:T(8,128)(2,1)}, bf16[64,128]{1,0:T(8,128)(2,1)}, u32[]{:S(2)}, u32[]{:S(2)}) collective-permute-start(bf16[64,128]{1,0:T(8,128)(2,1)} %get-tuple-element.116), channel_id=1, source_target_pairs={{0,1},{1,2},{2,3},{4,5},{5,6},{6,7},{8,9},{9,10},{10,11},{12,13},{... | collective-permute-start | bytes 49160 | tf_op jit(solution)/shard_map/ppermute | solution.py:10
  18.6 23.4 %collective-permute-start.3 = (bf16[128,128]{1,0:T(8,128)(2,1)}, bf16[128,128]{1,0:T(8,128)(2,1)S(1)}, u32[]{:S(2)}, u32[]{:S(2)}) collective-permute-start(bf16[128,128]{1,0:T(8,128)(2,1)} %get-tuple-element.113), channel_id=1, source_target_pairs={{4,0},{8,4},{12,8},{16,12},{20,16},{24,20},{28,24},{5,1},{9,5},{13... | collective-permute-start | bytes 98312 | tf_op jit(solution)/shard_map/ppermute | solution.py:10
  19.9 21.3 %collective-permute-start.2 = (bf16[128,128]{1,0:T(8,128)(2,1)}, bf16[128,128]{1,0:T(8,128)(2,1)}, u32[]{:S(2)}, u32[]{:S(2)}) collective-permute-start(bf16[128,128]{1,0:T(8,128)(2,1)} %get-tuple-element.114), channel_id=1, source_target_pairs={{0,4},{4,8},{8,12},{12,16},{16,20},{20,24},{24,28},{1,5},{5,9},{9,... | collective-permute-start | bytes 98312 | tf_op jit(solution)/shard_map/ppermute | solution.py:10
  32.3 33.3 %copy-start.41 = (bf16[3,256,128]{2,1,0:T(8,128)(2,1)}, bf16[3,256,128]{2,1,0:T(8,128)(2,1)S(1)}, u32[]{:S(2)}) copy-start(bf16[3,256,128]{2,1,0:T(8,128)(2,1)S(1)} %convert.42) | copy-start | bytes 589828
  67.1 21.9 %copy-start.88 = (f32[512]{0:T(512)}, f32[512]{0:T(512)S(1)}, u32[]{:S(2)}) copy-start(f32[512]{0:T(512)S(1)} %multiply_reduce_fusion.17) | copy-start | bytes 6148
  67.1 21.9 %copy-start.81 = (f32[512]{0:T(512)}, f32[512]{0:T(512)S(1)}, u32[]{:S(2)}) copy-start(f32[512]{0:T(512)S(1)} %fusion.145) | copy-start | bytes 6148
  68.1 22.5 %copy-start.25 = (bf16[512,128]{0,1:T(8,128)(2,1)}, bf16[512,128]{0,1:T(8,128)(2,1)S(1)}, u32[]{:S(2)}) copy-start(bf16[512,128]{0,1:T(8,128)(2,1)S(1)} %get-tuple-element.144) | copy-start | bytes 393220
  69.9 20.2 %collective-permute-start.7 = (bf16[128,128]{0,1:T(8,128)(2,1)S(1)}, bf16[128,128]{0,1:T(8,128)(2,1)}, u32[]{:S(2)}, u32[]{:S(2)}) collective-permute-start(bf16[128,128]{0,1:T(8,128)(2,1)S(1)} %get-tuple-element.109), channel_id=1, source_target_pairs={{4,0},{8,4},{12,8},{16,12},{20,16},{24,20},{28,24},{5,1},{9,5},{13... | collective-permute-start | bytes 98312 | tf_op jit(solution)/shard_map/ppermute | solution.py:10
  71.2 19.5 %collective-permute-start.6 = (bf16[128,128]{0,1:T(8,128)(2,1)S(1)}, bf16[128,128]{0,1:T(8,128)(2,1)}, u32[]{:S(2)}, u32[]{:S(2)}) collective-permute-start(bf16[128,128]{0,1:T(8,128)(2,1)S(1)} %get-tuple-element.110), channel_id=1, source_target_pairs={{0,4},{4,8},{8,12},{12,16},{16,20},{20,24},{24,28},{1,5},{5,9},{9,... | collective-permute-start | bytes 98312 | tf_op jit(solution)/shard_map/ppermute | solution.py:10
  76.5 13.5 %collective-permute-start.5 = (bf16[64,128]{0,1:T(8,128)(2,1)}, bf16[64,128]{0,1:T(8,128)(2,1)S(1)}, u32[]{:S(2)}, u32[]{:S(2)}) collective-permute-start(bf16[64,128]{0,1:T(8,128)(2,1)} %get-tuple-element.111), channel_id=1, source_target_pairs={{1,0},{2,1},{3,2},{5,4},{6,5},{7,6},{9,8},{10,9},{11,10},{13,12},{... | collective-permute-start | bytes 49160 | tf_op jit(solution)/shard_map/ppermute | solution.py:10
  79.2 10.8 %collective-permute-start.4 = (bf16[64,128]{0,1:T(8,128)(2,1)S(1)}, bf16[64,128]{0,1:T(8,128)(2,1)S(1)}, u32[]{:S(2)}, u32[]{:S(2)}) collective-permute-start(bf16[64,128]{0,1:T(8,128)(2,1)S(1)} %get-tuple-element.112), channel_id=1, source_target_pairs={{0,1},{1,2},{2,3},{4,5},{5,6},{6,7},{8,9},{9,10},{10,11},{12,13},{... | collective-permute-start | bytes 49160 | tf_op jit(solution)/shard_map/ppermute | solution.py:10
  122.9 22.4 %copy-start.13 = (f32[512,128]{0,1:T(8,128)}, f32[512,128]{0,1:T(8,128)S(1)}, u32[]{:S(2)}) copy-start(f32[512,128]{0,1:T(8,128)S(1)} %get-tuple-element.151) | copy-start | bytes 786436
  122.9 23.4 %copy-start.30 = (bf16[512,128]{0,1:T(8,128)(2,1)}, bf16[512,128]{0,1:T(8,128)(2,1)S(1)}, u32[]{:S(2)}) copy-start(bf16[512,128]{0,1:T(8,128)(2,1)S(1)} %get-tuple-element.150) | copy-start | bytes 393220
  125.9 20.3 %collective-permute-start.9 = (bf16[64,128]{0,1:T(8,128)(2,1)}, bf16[64,128]{0,1:T(8,128)(2,1)}, u32[]{:S(2)}, u32[]{:S(2)}) collective-permute-start(bf16[64,128]{0,1:T(8,128)(2,1)} %get-tuple-element.107), channel_id=1, source_target_pairs={{1,0},{2,1},{3,2},{5,4},{6,5},{7,6},{9,8},{10,9},{11,10},{13,12},{... | collective-permute-start | bytes 49160 | tf_op jit(solution)/shard_map/ppermute | solution.py:10
  127.9 18.4 %collective-permute-start.8 = (bf16[64,128]{0,1:T(8,128)(2,1)}, bf16[64,128]{0,1:T(8,128)(2,1)}, u32[]{:S(2)}, u32[]{:S(2)}) collective-permute-start(bf16[64,128]{0,1:T(8,128)(2,1)} %get-tuple-element.108), channel_id=1, source_target_pairs={{0,1},{1,2},{2,3},{4,5},{5,6},{6,7},{8,9},{9,10},{10,11},{12,13},{... | collective-permute-start | bytes 49160 | tf_op jit(solution)/shard_map/ppermute | solution.py:10
  131.5 14.8 %collective-permute-start.11 = (bf16[128,128]{0,1:T(8,128)(2,1)}, bf16[128,128]{0,1:T(8,128)(2,1)}, u32[]{:S(2)}, u32[]{:S(2)}) collective-permute-start(bf16[128,128]{0,1:T(8,128)(2,1)} %get-tuple-element.105), channel_id=1, source_target_pairs={{4,0},{8,4},{12,8},{16,12},{20,16},{24,20},{28,24},{5,1},{9,5},{13... | collective-permute-start | bytes 98312 | tf_op jit(solution)/shard_map/ppermute | solution.py:10
  132.8 13.5 %collective-permute-start.10 = (bf16[128,128]{0,1:T(8,128)(2,1)}, bf16[128,128]{0,1:T(8,128)(2,1)}, u32[]{:S(2)}, u32[]{:S(2)}) collective-permute-start(bf16[128,128]{0,1:T(8,128)(2,1)} %get-tuple-element.106), channel_id=1, source_target_pairs={{0,4},{4,8},{8,12},{12,16},{16,20},{20,24},{24,28},{1,5},{5,9},{9,... | collective-permute-start | bytes 98312 | tf_op jit(solution)/shard_map/ppermute | solution.py:10
  138.0 46.4 %copy-start.5 = (f32[512,128]{0,1:T(8,128)}, f32[512,128]{0,1:T(8,128)S(1)}, u32[]{:S(2)}) copy-start(f32[512,128]{0,1:T(8,128)S(1)} %copy.95) | copy-start | bytes 786436
  227.3 41.0 %collective-permute-start.12 = (bf16[64,128]{1,0:T(8,128)(2,1)}, bf16[64,128]{1,0:T(8,128)(2,1)}, u32[]{:S(2)}, u32[]{:S(2)}) collective-permute-start(bf16[64,128]{1,0:T(8,128)(2,1)} %get-tuple-element.101), channel_id=1, source_target_pairs={{0,1},{1,2},{2,3},{4,5},{5,6},{6,7},{8,9},{9,10},{10,11},{12,13},{... | collective-permute-start | bytes 49160 | tf_op jit(solution)/shard_map/ppermute | solution.py:10
  229.5 38.8 %collective-permute-start.13 = (bf16[64,128]{1,0:T(8,128)(2,1)}, bf16[64,128]{1,0:T(8,128)(2,1)}, u32[]{:S(2)}, u32[]{:S(2)}) collective-permute-start(bf16[64,128]{1,0:T(8,128)(2,1)} %get-tuple-element.102), channel_id=1, source_target_pairs={{1,0},{2,1},{3,2},{5,4},{6,5},{7,6},{9,8},{10,9},{11,10},{13,12},{... | collective-permute-start | bytes 49160 | tf_op jit(solution)/shard_map/ppermute | solution.py:10
  232.2 36.1 %collective-permute-start.14 = (bf16[128,128]{1,0:T(8,128)(2,1)}, bf16[128,128]{1,0:T(8,128)(2,1)}, u32[]{:S(2)}, u32[]{:S(2)}) collective-permute-start(bf16[128,128]{1,0:T(8,128)(2,1)} %get-tuple-element.103), channel_id=1, source_target_pairs={{0,4},{4,8},{8,12},{12,16},{16,20},{20,24},{24,28},{1,5},{5,9},{9,... | collective-permute-start | bytes 98312 | tf_op jit(solution)/shard_map/ppermute | solution.py:10
  236.5 31.8 %collective-permute-start.15 = (bf16[128,128]{1,0:T(8,128)(2,1)}, bf16[128,128]{1,0:T(8,128)(2,1)}, u32[]{:S(2)}, u32[]{:S(2)}) collective-permute-start(bf16[128,128]{1,0:T(8,128)(2,1)} %get-tuple-element.104), channel_id=1, source_target_pairs={{4,0},{8,4},{12,8},{16,12},{20,16},{24,20},{28,24},{5,1},{9,5},{13... | collective-permute-start | bytes 98312 | tf_op jit(solution)/shard_map/ppermute | solution.py:10
  237.8 26.1 %copy-start.32 = (f32[512,128]{0,1:T(8,128)S(1)}, f32[512,128]{0,1:T(8,128)}, u32[]{:S(2)}) copy-start(f32[512,128]{0,1:T(8,128)} %fusion.3) | copy-start | bytes 786436
  249.7 21.9 %copy-start.12 = (f32[512,128]{0,1:T(8,128)S(1)}, f32[512,128]{0,1:T(8,128)}, u32[]{:S(2)}) copy-start(f32[512,128]{0,1:T(8,128)} %copy-done.11) | copy-start | bytes 786436
  249.7 21.9 %copy-start.80 = (f32[512]{0:T(512)S(1)}, f32[512]{0:T(512)}, u32[]{:S(2)}) copy-start(f32[512]{0:T(512)} %copy-done.79) | copy-start | bytes 6148
  249.8 21.9 %copy-start.83 = (f32[512]{0:T(512)S(1)}, f32[512]{0:T(512)}, u32[]{:S(2)}) copy-start(f32[512]{0:T(512)} %copy-done.82) | copy-start | bytes 6148
  249.8 21.9 %copy-start.99 = (f32[128]{0:T(128)S(1)}, f32[128]{0:T(128)}, u32[]{:S(2)}) copy-start(f32[128]{0:T(128)} %get-tuple-element.124) | copy-start | bytes 1540
  328.1 32.8 %copy-start.10 = (f32[512,128]{0,1:T(8,128)S(1)}, f32[512,128]{0,1:T(8,128)}, u32[]{:S(2)}) copy-start(f32[512,128]{0,1:T(8,128)} %copy-done.9) | copy-start | bytes 786436
  329.1 28.7 %collective-permute-start.16 = (bf16[64,128]{1,0:T(8,128)(2,1)}, bf16[64,128]{1,0:T(8,128)(2,1)S(1)}, u32[]{:S(2)}, u32[]{:S(2)}) collective-permute-start(bf16[64,128]{1,0:T(8,128)(2,1)} %get-tuple-element.97), channel_id=1, source_target_pairs={{0,1},{1,2},{2,3},{4,5},{5,6},{6,7},{8,9},{9,10},{10,11},{12,13},{... | collective-permute-start | bytes 49160 | tf_op jit(solution)/shard_map/ppermute | solution.py:10
  332.5 25.3 %collective-permute-start.17 = (bf16[64,128]{1,0:T(8,128)(2,1)}, bf16[64,128]{1,0:T(8,128)(2,1)S(1)}, u32[]{:S(2)}, u32[]{:S(2)}) collective-permute-start(bf16[64,128]{1,0:T(8,128)(2,1)} %get-tuple-element.98), channel_id=1, source_target_pairs={{1,0},{2,1},{3,2},{5,4},{6,5},{7,6},{9,8},{10,9},{11,10},{13,12},{... | collective-permute-start | bytes 49160 | tf_op jit(solution)/shard_map/ppermute | solution.py:10
  334.5 23.4 %collective-permute-start.18 = (bf16[128,128]{1,0:T(8,128)(2,1)}, bf16[128,128]{1,0:T(8,128)(2,1)S(1)}, u32[]{:S(2)}, u32[]{:S(2)}) collective-permute-start(bf16[128,128]{1,0:T(8,128)(2,1)} %get-tuple-element.99), channel_id=1, source_target_pairs={{0,4},{4,8},{8,12},{12,16},{16,20},{20,24},{24,28},{1,5},{5,9},{9,... | collective-permute-start | bytes 98312 | tf_op jit(solution)/shard_map/ppermute | solution.py:10
  338.7 19.1 %collective-permute-start.19 = (bf16[128,128]{1,0:T(8,128)(2,1)}, bf16[128,128]{1,0:T(8,128)(2,1)S(1)}, u32[]{:S(2)}, u32[]{:S(2)}) collective-permute-start(bf16[128,128]{1,0:T(8,128)(2,1)} %get-tuple-element.100), channel_id=1, source_target_pairs={{4,0},{8,4},{12,8},{16,12},{20,16},{24,20},{28,24},{5,1},{9,5},{13... | collective-permute-start | bytes 98312 | tf_op jit(solution)/shard_map/ppermute | solution.py:10
  417.7 11.5 %collective-permute-start.20 = (bf16[64,128]{1,0:T(8,128)(2,1)S(1)}, bf16[64,128]{1,0:T(8,128)(2,1)S(1)}, u32[]{:S(2)}, u32[]{:S(2)}) collective-permute-start(bf16[64,128]{1,0:T(8,128)(2,1)S(1)} %get-tuple-element.93), channel_id=1, source_target_pairs={{0,1},{1,2},{2,3},{4,5},{5,6},{6,7},{8,9},{9,10},{10,11},{12,13},{... | collective-permute-start | bytes 49160 | tf_op jit(solution)/shard_map/ppermute | solution.py:10
  421.6 7.6 %collective-permute-start.21 = (bf16[64,128]{1,0:T(8,128)(2,1)S(1)}, bf16[64,128]{1,0:T(8,128)(2,1)S(1)}, u32[]{:S(2)}, u32[]{:S(2)}) collective-permute-start(bf16[64,128]{1,0:T(8,128)(2,1)S(1)} %get-tuple-element.94), channel_id=1, source_target_pairs={{1,0},{2,1},{3,2},{5,4},{6,5},{7,6},{9,8},{10,9},{11,10},{13,12},{... | collective-permute-start | bytes 49160 | tf_op jit(solution)/shard_map/ppermute | solution.py:10
  423.6 5.6 %collective-permute-start.22 = (bf16[128,128]{1,0:T(8,128)(2,1)S(1)}, bf16[128,128]{1,0:T(8,128)(2,1)S(1)}, u32[]{:S(2)}, u32[]{:S(2)}) collective-permute-start(bf16[128,128]{1,0:T(8,128)(2,1)S(1)} %get-tuple-element.95), channel_id=1, source_target_pairs={{0,4},{4,8},{8,12},{12,16},{16,20},{20,24},{24,28},{1,5},{5,9},{9,... | collective-permute-start | bytes 98312 | tf_op jit(solution)/shard_map/ppermute | solution.py:10
  427.9 4.7 collective-permute-start.23
  435.4 99.7 %copy-start.49 = (f32[512,128]{1,0:T(8,128)}, f32[512,128]{1,0:T(8,128)S(1)}, u32[]{:S(2)}) copy-start(f32[512,128]{1,0:T(8,128)S(1)} %scatter_custom_fusion.11) | copy-start | bytes 786436
  (108 other events, 585.1 us)
Sparse Core Ops, SparseCore 0:
  393.9 135.6 all-reduce.1
where the time goes:
time: 559 us; the launch traced here: 548 us
  local copies, waits for them, and re-layouts  161 us (29%)
  other arithmetic  151 us (27%)
  waiting for transfers between devices  97.5 us (17%)
  starting transfers between devices  69.4 us (12%)
  matrix products  52.3 us (9%)
  between operations  16.9 us (3%)
    psum x1, waiting for transfers between devices, on_device(): stacked = lax.psum(stacked, ('dom', 'sub'))  94.2 us
    ppermute x24, starting transfers between devices, passed_along(): lax.ppermute(value, axis, [(source, source + steps) for source in range(f...  69.3 us
    scatter-add x3, other arithmetic, layer_local(): jax.ops.segment_sum(message, receivers, num_segments=latent.shape[0])  36.7 us
    unnamed x299, local copies, waits for them, and re-layouts  36.6 us
    scatter-add x3, other arithmetic, layer_local(): extended[senders]  35.8 us
    scatter-add x3, other arithmetic, layer_local(): own[receivers]  35.6 us
    gather x6, local copies, waits for them, and re-layouts, layer_local(): jax.ops.segment_sum(message, receivers, num_segments=latent.shape[0])  31 us
    gather x5, local copies, waits for them, and re-layouts, layer_local(): extended[senders]  21.6 us
  transfers between devices with their start and end apart: 25, of which 2 were waited for; matrix products, arithmetic and copies ran while one was open for 20% of the time, Pallas kernels for 0%

commit v1 on v0

v1 whole, which is shorter than its diff:
```python
import functools

import jax
import jax.numpy as jnp
from jax import lax
from jax.experimental import pallas as pl
from jax.experimental.pallas import tpu as pltpu
from jax.sharding import PartitionSpec as P

F32 = jnp.float32
BF16 = jnp.bfloat16
EPS = 1e-05


def mm(a, b):
    return jnp.dot(a, b, preferred_element_type=F32)


def mm_tn(a, b):
    return lax.dot_general(a, b, (((0,), (0,)), ((), ())), preferred_element_type=F32)


def mm_nt(a, b):
    return lax.dot_general(a, b, (((1,), (1,)), ((), ())), preferred_element_type=F32)


def rsum(v):
    return jnp.sum(v, axis=0, keepdims=True)


def lmean(v):
    return jnp.mean(v, axis=-1, keepdims=True)


def remote(src, dst, send_sem, recv_sem, device):
    return pltpu.make_async_remote_copy(
        src_ref=src,
        dst_ref=dst,
        send_sem=send_sem,
        recv_sem=recv_sem,
        device_id=device,
        device_id_type=pl.DeviceIdType.MESH,
    )


def as_column(row):
    width = row.shape[1]
    eye = lax.broadcasted_iota(jnp.int32, (width, width), 0) == lax.broadcasted_iota(
        jnp.int32, (width, width), 1
    )
    return jnp.sum(jnp.where(eye, row.astype(F32), 0.0), axis=1, keepdims=True)


def silu_parts(x):
    sig = 0.5 * jnp.tanh(0.5 * x) + 0.5
    return x * sig, sig * (1.0 + x * (1.0 - sig))


def kernel(dims, *refs):
    nd, ns, layers, n, e, sr, D, te, r2 = dims
    (nodes, edges, snd, rcv, live, flags, send,
     w1, b1, w2, o1, g1, wn, nb, wn2, no, ng, wo, gout,
     out_l, out_g, q_w1, q_b1, q_w2, q_o1, q_g1, q_wn, q_nb, q_wn2, q_no, q_ng, q_wo,
     ohs, ohst, ohr, ohrt, ohx, ohxt, fcol,
     c_w1, c_w2, c_wn, c_wn2, c_wo,
     joined, act, ds1, xhat, rstd, estate, summed,
     nin, hid, dsn, nxhat, nrstd, lat,
     sent, halo, hgrad, ret,
     dedge, dp1, dp2, dext, dsh, glat, acc1, acc2, bacc,
     flat, r1, f2, rr2, g3, g4, br1, bs1, br2,
     hs_s, hs_r, hb_s, hb_r, q1s, q1r, q2s, q2r, q3s, q3r, q4s, q4r, bq1s, bq1r, bq2s, bq2r,
     ) = refs
    d = lax.axis_index("dom")
    s = lax.axis_index("sub")
    low, high = sr // 6, sr // 3
    c1 = nd * r2
    tiles = e // te
    hid_rows = w2.shape[1]
    k1 = w1.shape[1]
    kn = wn.shape[1]

    halo[...] = jnp.zeros_like(halo)
    ret[...] = jnp.zeros_like(ret)

    barrier = pltpu.get_barrier_semaphore()
    for k in range(1, ns):
        pl.semaphore_signal(barrier, inc=1, device_id=(d, lax.rem(s + k, ns)),
                            device_id_type=pl.DeviceIdType.MESH)
    for k in range(1, nd):
        pl.semaphore_signal(barrier, inc=1, device_id=(lax.rem(d + k, nd), s),
                            device_id_type=pl.DeviceIdType.MESH)
    pl.semaphore_wait(barrier, ns - 1 + nd - 1)

    S_rows = [(low, low), (0, low), (2 * low + high, high), (2 * low, high)]
    H_rows = [(0, low), (low, low), (2 * low, high), (2 * low + high, high)]
    has_next = [s < ns - 1, s > 0, d < nd - 1, d > 0]
    has_prev = [s > 0, s < ns - 1, d > 0, d < nd - 1]
    nxt = [(d, jnp.minimum(s + 1, ns - 1)), (d, jnp.maximum(s - 1, 0)),
           (jnp.minimum(d + 1, nd - 1), s), (jnp.maximum(d - 1, 0), s)]
    prv = [nxt[1], nxt[0], nxt[3], nxt[2]]

    def part(ref, layer, rows):
        return ref.at[layer, pl.ds(rows[0], rows[1])]

    def halo_copy(layer, i):
        return remote(part(sent, layer, S_rows[i]), part(halo, layer, H_rows[i]),
                      hs_s.at[layer, i], hs_r.at[layer, i], nxt[i])

    def back_copy(layer, i):
        return remote(part(hgrad, layer, H_rows[i]), part(ret, layer, S_rows[i]),
                      hb_s.at[layer, i], hb_r.at[layer, i], prv[i])

    def start_moves(make, layer, sends):
        for i in range(4):
            @pl.when(sends[i])
            def _(i=i):
                make(layer, i).start()

    def wait_moves(make, layer, sends, recvs):
        for i in range(4):
            @pl.when(recvs[i])
            def _(i=i):
                make(layer, i).wait_recv()
        for i in range(4):
            @pl.when(sends[i])
            def _(i=i):
                make(layer, i).wait_send()

    def build(ids, count, oh, oht, mask):
        width = oh.shape[1]

        def body(r, carry):
            row = ids[pl.ds(r, 1), :]
            if mask is not None:
                row = jnp.where(mask[pl.ds(r, 1), :] > 0, row, -1)
            at = pl.multiple_of(r * 128, 128)
            down = lax.broadcasted_iota(jnp.int32, (width, 128), 0)
            oht[:, pl.ds(at, 128)] = jnp.where(down == row, 1.0, 0.0).astype(BF16)
            col = as_column(row).astype(jnp.int32)
            across = lax.broadcasted_iota(jnp.int32, (128, width), 1)
            oh[pl.ds(at, 128), :] = jnp.where(across == col, 1.0, 0.0).astype(BF16)
            return carry

        lax.fori_loop(0, count // 128, body, 0)

    build(send, sr, ohx, ohxt, None)

    lat[...] = nodes[...].astype(F32)

    def start_layer(layer):
        own = lat[...].astype(BF16)
        nin[layer, :, 0:D] = own
        sent[layer] = mm(ohx[...], own).astype(BF16)
        start_moves(halo_copy, layer, has_next)

    start_layer(0)
    build(snd, e, ohs, ohst, None)
    build(rcv, e, ohr, ohrt, live)

    def flag_body(r, carry):
        at = pl.multiple_of(r * 128, 128)
        fcol[pl.ds(at, 128), :] = as_column(flags[pl.ds(r, 1), :])
        return carry

    lax.fori_loop(0, n // 128, flag_body, 0)
    for layer in range(layers):
        c_w1[layer] = w1[layer].astype(BF16)
        c_w2[layer] = w2[layer].astype(BF16)
        c_wn[layer] = wn[layer].astype(BF16)
        c_wn2[layer] = wn2[layer].astype(BF16)
        c_wo[layer] = wo[layer].astype(BF16)
    bacc[...] = jnp.zeros_like(bacc)
    estate[...] = edges[...].astype(F32)
    pad = flat.shape[1] - (k1 + hid_rows + kn + 2 * D)
    if pad:
        for layer in range(layers):
            flat[layer, pl.ds(k1 + hid_rows + kn + 2 * D, pad), :] = jnp.zeros((pad, D), BF16)

    for layer in range(layers):
        own = nin[layer, :, 0:D]

        def local(t, carry, layer=layer):
            rows = pl.ds(pl.multiple_of(t * te, te), te)
            own = nin[layer, :, 0:D]
            joined[layer, rows, 0:D] = estate[rows, :].astype(BF16)
            joined[layer, rows, D:2 * D] = mm(ohs[rows, 0:n], own).astype(BF16)
            joined[layer, rows, 2 * D:3 * D] = mm(ohr[rows, :], own).astype(BF16)
            return carry

        lax.fori_loop(0, tiles, local, 0)
        summed[...] = jnp.zeros_like(summed)
        wait_moves(halo_copy, layer, has_next, has_prev)

        def edge(t, carry, layer=layer):
            rows = pl.ds(pl.multiple_of(t * te, te), te)
            far = mm(ohs[rows, n:], halo[layer])
            xs = (joined[layer, rows, D:2 * D].astype(F32) + far).astype(BF16)
            joined[layer, rows, D:2 * D] = xs
            pre = mm(joined[layer, rows, :], c_w1[layer]) + b1[pl.ds(layer, 1), :]
            a, da = silu_parts(pre)
            a = a.astype(BF16)
            act[layer, rows, :] = a
            ds1[layer, rows, :] = da
            two = mm(a, c_w2[layer]) + o1[pl.ds(layer, 1), :]
            cen = two - lmean(two)
            rs = lax.rsqrt(lmean(cen * cen) + EPS)
            xh = cen * rs
            xhat[layer, rows, :] = xh
            rstd[layer, rows, :] = rs
            msg = g1[pl.ds(layer, 1), :] * xh
            estate[rows, :] += msg
            summed[...] += mm(ohrt[:, rows], msg.astype(BF16))
            return carry

        lax.fori_loop(0, tiles, edge, 0)

        sh = summed[...].astype(BF16)
        nin[layer, :, D:2 * D] = sh
        pre = mm(nin[layer], c_wn[layer]) + nb[pl.ds(layer, 1), :]
        a, da = silu_parts(pre)
        a = a.astype(BF16)
        hid[layer] = a
        dsn[layer] = da
        two = mm(a, c_wn2[layer]) + no[pl.ds(layer, 1), :]
        cen = two - lmean(two)
        rs = lax.rsqrt(lmean(cen * cen) + EPS)
        xh = cen * rs
        nxhat[layer] = xh
        nrstd[layer] = rs
        lat[...] = lat[...] + ng[pl.ds(layer, 1), :] * xh + fcol[...] * mm(sh, c_wo[layer])
        if layer + 1 < layers:
            start_layer(layer + 1)
    out_l[...] = lat[...]

    def s1(layer, k):
        peer = lax.rem(s + k, ns)
        return remote(flat.at[layer, pl.ds(pl.multiple_of(peer * c1, 16), c1)], r1.at[layer, s],
                      q1s.at[layer, k], q1r.at[layer, k], (d, peer))

    def s2(layer, k):
        peer = lax.rem(d + k, nd)
        return remote(f2.at[layer, pl.ds(pl.multiple_of(peer * r2, 16), r2)], rr2.at[layer, d],
                      q2s.at[layer, k], q2r.at[layer, k], (peer, s))

    def s3(layer, k):
        peer = lax.rem(d + k, nd)
        mine = g3.at[layer, pl.ds(pl.multiple_of(d * r2, 16), r2)]
        return remote(mine, mine, q3s.at[layer, k], q3r.at[layer, k], (peer, s))

    def s4(layer, k):
        peer = lax.rem(s + k, ns)
        return remote(g3.at[layer], g4.at[layer, pl.ds(pl.multiple_of(s * c1, 16), c1)],
                      q4s.at[layer, k], q4r.at[layer, k], (d, peer))

    def bias1(layer, k):
        return remote(bacc, br1.at[s], bq1s.at[k], bq1r.at[k], (d, lax.rem(s + k, ns)))

    def bias2(layer, k):
        return remote(bs1, br2.at[d], bq2s.at[k], bq2r.at[k], (lax.rem(d + k, nd), s))

    def start_all(make, layer, count):
        for k in range(1, count):
            make(layer, k).start()

    def wait_all(make, layer, count):
        for k in range(1, count):
            make(layer, k).wait_recv()
        for k in range(1, count):
            make(layer, k).wait_send()

    def stage1(layer):
        start_all(s1, layer, ns)

    def stage2(layer):
        r1[layer, s] = flat[layer, pl.ds(pl.multiple_of(s * c1, 16), c1), :]
        wait_all(s1, layer, ns)
        total = r1[layer, 0].astype(F32)
        for j in range(1, ns):
            total = total + r1[layer, j].astype(F32)
        f2[layer] = total.astype(BF16)
        start_all(s2, layer, nd)

    def stage3(layer):
        rr2[layer, d] = f2[layer, pl.ds(pl.multiple_of(d * r2, 16), r2), :]
        wait_all(s2, layer, nd)
        total = rr2[layer, 0].astype(F32)
        for j in range(1, nd):
            total = total + rr2[layer, j].astype(F32)
        g3[layer, pl.ds(pl.multiple_of(d * r2, 16), r2), :] = total.astype(BF16)
        start_all(s3, layer, nd)

    def stage4(layer):
        wait_all(s3, layer, nd)
        start_all(s4, layer, ns)
        g4[layer, pl.ds(pl.multiple_of(s * c1, 16), c1), :] = g3[layer]

    def stage5(layer):
        wait_all(s4, layer, ns)
        at = 0
        for out, count in ((q_w1, k1), (q_w2, hid_rows), (q_wn, kn), (q_wn2, D), (q_wo, D)):
            out[layer] = g4[layer, pl.ds(at, count), :].astype(F32)
            at += count

    def norm_back(dxh, xh, rs):
        return rs * (dxh - lmean(dxh) - xh * lmean(dxh * xh))

    glat[...] = gout[...]
    dedge[...] = jnp.zeros_like(dedge)
    for layer in reversed(range(layers)):
        row = layer * 6
        g = glat[...]
        xh = nxhat[layer]
        bacc[pl.ds(row + 5, 1), :] = rsum(g * xh)
        dtwo = norm_back(g * ng[pl.ds(layer, 1), :], xh, nrstd[layer])
        bacc[pl.ds(row + 4, 1), :] = rsum(dtwo)
        dtwo = dtwo.astype(BF16)
        dh = mm_nt(dtwo, c_wn2[layer]).astype(BF16).astype(F32)
        dpre = dh * dsn[layer]
        bacc[pl.ds(row + 3, 1), :] = rsum(dpre)
        dpre = dpre.astype(BF16)
        dout = (fcol[...] * g).astype(BF16)
        dnin = mm_nt(dpre, c_wn[layer])
        dsum = dnin[:, D:].astype(BF16).astype(F32) + mm_nt(dout, c_wo[layer]).astype(BF16).astype(F32)
        dsh[...] = dsum.astype(BF16)
        dext[...] = jnp.zeros_like(dext)
        glat[...] = g + dnin[:, :D]

        def edge_back(t, carry, layer=layer, row=row):
            rows = pl.ds(pl.multiple_of(t * te, te), te)
            dmsg = dedge[rows, :] + mm(ohr[rows, :], dsh[...])
            xh = xhat[layer, rows, :]
            bacc[pl.ds(row + 2, 1), :] += rsum(dmsg * xh)
            dtwo = norm_back(dmsg * g1[pl.ds(layer, 1), :], xh, rstd[layer, rows, :])
            bacc[pl.ds(row + 1, 1), :] += rsum(dtwo)
            dtwo = dtwo.astype(BF16)
            dp2[rows, :] = dtwo
            da = mm_nt(dtwo, c_w2[layer]).astype(BF16).astype(F32)
            dpre = da * ds1[layer, rows, :]
            bacc[pl.ds(row, 1), :] += rsum(dpre)
            dpre = dpre.astype(BF16)
            dp1[rows, :] = dpre
            dj = mm_nt(dpre, c_w1[layer]).astype(BF16)
            dext[...] += mm(ohst[:, rows], dj[:, D:2 * D])
            glat[...] += mm(ohrt[:, rows], dj[:, 2 * D:])
            if layer > 0:
                dedge[rows, :] += dj[:, 0:D].astype(F32)
            return carry

        lax.fori_loop(0, tiles, edge_back, 0)
        hgrad[layer] = dext[n:, :].astype(BF16)
        start_moves(back_copy, layer, has_prev)

        acc1[...] = jnp.zeros_like(acc1)
        acc2[...] = jnp.zeros_like(acc2)

        def grads(t, carry, layer=layer):
            rows = pl.ds(pl.multiple_of(t * te, te), te)
            acc1[...] += mm_tn(joined[layer, rows, :], dp1[rows, :])
            acc2[...] += mm_tn(act[layer, rows, :], dp2[rows, :])
            return carry

        lax.fori_loop(0, tiles, grads, 0)
        at = 0
        for value in (acc1[...], acc2[...], mm_tn(nin[layer], dpre),
                      mm_tn(hid[layer], dtwo), mm_tn(nin[layer, :, D:2 * D], dout)):
            count = value.shape[0]
            flat[layer, pl.ds(at, count), :] = value.astype(BF16)
            at += count
        stage1(layer)
        if layer == 0:
            start_all(bias1, 0, ns)
        if layer + 1 < layers:
            stage2(layer + 1)
        if layer + 2 < layers:
            stage4(layer + 2)
        glat[...] += dext[0:n, :]
        wait_moves(back_copy, layer, has_prev, has_next)
        glat[...] += mm(ohxt[...], ret[layer])
        if layer + 1 < layers:
            stage3(layer + 1)
        if layer + 2 < layers:
            stage5(layer + 2)
    out_g[...] = glat[...]

    stage2(0)
    br1[s] = bacc[...]
    wait_all(bias1, 0, ns)
    total = br1[0]
    for j in range(1, ns):
        total = total + br1[j]
    bs1[...] = total
    start_all(bias2, 0, nd)
    if layers > 1:
        stage4(1)
    stage3(0)
    br2[d] = bs1[...]
    wait_all(bias2, 0, nd)
    total = br2[0]
    for j in range(1, nd):
        total = total + br2[j]
    for layer in range(layers):
        for i, out in enumerate((q_b1, q_o1, q_g1, q_nb, q_no, q_ng)):
            out[pl.ds(layer, 1), :] = total[layer * 6 + i:layer * 6 + i + 1, :]
    stage4(0)
    if layers > 1:
        stage5(1)
    stage5(0)


def on_device(nd, ns, nodes, edges, senders, receivers, edge_live, outlet_flags, send_rows, *rest):
    weights, grad_out = rest[:-1], rest[-1]
    n, D = nodes.shape
    e = edges.shape[0]
    sr = send_rows.shape[0]
    layers = weights[0].shape[0]
    te = min(512, e)
    grad_rows = sum(w.shape[1] for w in weights if w.ndim == 3)
    r2 = pl.cdiv(grad_rows, ns * nd * 16) * 16
    c1 = nd * r2
    total = ns * c1
    brows = pl.cdiv(6 * layers, 8) * 8
    ext = n + sr
    dims = (nd, ns, layers, n, e, sr, D, te, r2)
    V = pltpu.VMEM
    scratch = [
        V((e, ext), BF16), V((ext, e), BF16), V((e, n), BF16), V((n, e), BF16),
        V((sr, n), BF16), V((n, sr), BF16), V((n, 1), F32),
        V(weights[0].shape, BF16), V(weights[2].shape, BF16), V(weights[5].shape, BF16),
        V(weights[7].shape, BF16), V(weights[10].shape, BF16),
        V((layers, e, 3 * D), BF16), V((layers, e, D), BF16), V((layers, e, D), F32),
        V((layers, e, D), F32), V((layers, e, 1), F32), V((e, D), F32), V((n, D), F32),
        V((layers, n, 2 * D), BF16), V((layers, n, D), BF16), V((layers, n, D), F32),
        V((layers, n, D), F32), V((layers, n, 1), F32), V((n, D), F32),
        V((layers, sr, D), BF16), V((layers, sr, D), BF16), V((layers, sr, D), BF16),
        V((layers, sr, D), BF16),
        V((e, D), F32), V((e, D), BF16), V((e, D), BF16), V((ext, D), F32), V((n, D), BF16),
        V((n, D), F32), V((3 * D, D), F32), V((D, D), F32), V((brows, D), F32),
        V((layers, total, D), BF16), V((layers, ns, c1, D), BF16), V((layers, c1, D), BF16),
        V((layers, nd, r2, D), BF16), V((layers, c1, D), BF16), V((layers, total, D), BF16),
        V((ns, brows, D), F32), V((brows, D), F32), V((nd, brows, D), F32),
    ]
    sem = pltpu.SemaphoreType.DMA
    scratch += [sem((layers, 4))] * 4
    scratch += [sem((layers, ns))] * 2 + [sem((layers, nd))] * 4 + [sem((layers, ns))] * 2
    scratch += [sem((ns,))] * 2 + [sem((nd,))] * 2
    shapes = [jax.ShapeDtypeStruct((n, D), F32)] * 2 + [
        jax.ShapeDtypeStruct(w.shape, F32) for w in weights
    ]
    vmem = pl.BlockSpec(memory_space=pltpu.VMEM)
    rows = lambda v: v.reshape(-1, 128)
    args = (nodes, edges, rows(senders), rows(receivers), rows(edge_live), rows(outlet_flags),
            rows(send_rows), *weights, grad_out)
    return tuple(pl.pallas_call(
        functools.partial(kernel, dims),
        out_shape=shapes,
        in_specs=[vmem] * len(args),
        out_specs=[vmem] * len(shapes),
        scratch_shapes=scratch,
        compiler_params=pltpu.CompilerParams(
            collective_id=0, has_side_effects=True, vmem_limit_bytes=60 * 1024 * 1024
        ),
    )(*args))


def solution(mesh):
    split = ("dom", "sub")
    placed = (P(split, None),) * 2 + (P(split),) * 5 + (P(),) * 11 + (P(split, None),)
    return jax.shard_map(
        functools.partial(on_device, mesh.shape["dom"], mesh.shape["sub"]),
        mesh=mesh,
        in_specs=placed,
        out_specs=(P(split, None),) * 2 + (P(),) * 11,
        check_vma=False,
    )
```

time: 559 us -> 101 us (0.18); the launches traced: 548 us -> 101 us
  other arithmetic: 151 us -> 0 us
  local copies, waits for them, and re-layouts: 161 us -> 10.7 us
  waiting for transfers between devices: 97.5 us -> 0 us
  Pallas kernels: 0 us -> 89.7 us
  starting transfers between devices: 69.4 us -> 0 us
  matrix products: 52.3 us -> 0 us
  between operations: 16.9 us -> 0.69 us
    scatter-add x12 -> x0, other arithmetic: 117 us -> none  [the longest x3 36.7 us: layer_local(): jax.ops.segment_sum(message, receivers, num_segments=latent.shape[0])]
    psum x1 -> x0, waiting for transfers between devices: 94.2 us -> none  [on_device(): stacked = lax.psum(stacked, ('dom', 'sub'))]
    pallas_call x0 -> x1, Pallas kernels: none -> 89.7 us  [on_device(): pl.pallas_call(functools.partial(kernel, dims), out_shape=shapes, in_spec...]
    gather x21 -> x0, local copies, waits for them, and re-layouts: 78.8 us -> none  [the longest x6 31 us: layer_local(): jax.ops.segment_sum(message, receivers, num_segments=latent.shape[0])]
    ppermute x24 -> x0, starting transfers between devices: 69.3 us -> none  [passed_along(): lax.ppermute(value, axis, [(source, source + steps) for source in range(f...]
    dot_general x45 -> x0, matrix products: 52.3 us -> none  [the longest x9 12.3 us: layer_local(): jnp.dot(act_one, edge_second.astype(jnp.bfloat16), preferred_element_type...]
    unnamed x299 -> x35, local copies, waits for them, and re-layouts: 36.6 us -> 10.7 us
    reduce_sum x24 -> x0, other arithmetic: 16.3 us -> none  [the longest x3 6.23 us: layer_local(): message = live[:, None] * (edge_gain * normalize(pre_two))]
  transfers between devices with their start and end apart: 25 -> 0, of which waited for: 2 -> 0; matrix products, arithmetic and copies ran while one was open for 20% -> 0% of each run, Pallas kernels for 0% -> 0%
where the time goes in v1:
time: 101 us
  Pallas kernels  89.7 us (89%)
  local copies, waits for them, and re-layouts  10.7 us (11%)
    pallas_call x1, Pallas kernels, on_device(): pl.pallas_call(functools.partial(kernel, dims), out_shape=shapes, in_spec...  89.7 us
    unnamed x35, local copies, waits for them, and re-layouts  10.7 us

profile of v1, /device:TPU:1, one launch (start us, length us, event | category | flops | bytes accessed | tf_op | source)
XLA Modules:
  0.0 101.1 jit_solution(988796005891999378)
XLA Ops:
  0.7 89.7 %shard_map.282 = (f32[512,128]{1,0:T(8,128)}, f32[512,128]{1,0:T(8,128)}, f32[3,384,128]{2,1,0:T(8,128)}, f32[3,128]{1,0:T(4,128)}, f32[3,128,128]{2,1,0:T(8,128...) custom-call(bf16[512,128]{1,0:T(8,128)(2,1)} %refs_0_.1, ...), custom_call_target="tpu_custom_call" | custom-call | tf_op jit(solution)/shard_map/pallas_call | solution.py:453
  90.4 0.0 copy-start
  90.4 1.7 %copy.45 = f32[512,128]{1,0:T(8,128)} copy(f32[512,128]{1,0:T(8,128)} %get-tuple-element.26) | data formatting | bytes 524288
  92.1 1.7 %copy.46 = f32[512,128]{1,0:T(8,128)} copy(f32[512,128]{1,0:T(8,128)} %get-tuple-element.27) | data formatting | bytes 524288
  93.8 0.0 copy-done
  93.8 0.0 copy-start.10
  93.8 0.0 copy-start.4
  93.8 0.8 copy.47
  94.6 0.0 copy-done.10
  94.6 0.0 copy-start.1
  94.6 0.6 copy.48
  95.2 0.0 copy-done.4
  95.2 0.0 copy-start.9
  95.2 0.7 copy.49
  95.9 0.0 copy-done.9
  95.9 0.0 copy-start.8
  95.9 0.6 copy.50
  96.5 0.1 copy-done.8
  96.6 0.6 copy.51
  97.2 0.0 copy-done.1
  97.2 0.0 copy-start.7
  97.2 0.0 copy-start.3
  97.2 0.7 copy.52
  97.9 0.0 copy-done.7
  97.9 0.6 copy.53
  98.5 0.0 copy-done.3
  98.5 0.0 copy-start.6
  98.5 0.0 copy-start.2
  98.5 0.7 copy.54
  99.2 0.0 copy-done.6
  99.2 0.0 copy-start.5
  99.2 0.6 copy.55
  99.8 0.1 copy-done.5
  99.9 0.6 copy.56
  100.4 0.0 copy-done.2
  100.4 0.7 copy.57
Async XLA Ops:
  90.4 3.4 %copy-start = (f32[3,384,128]{2,1,0:T(8,128)S(1)}, f32[3,384,128]{2,1,0:T(8,128)}, u32[]{:S(2)}) copy-start(f32[3,384,128]{2,1,0:T(8,128)} %get-tuple-element.28) | copy-start | bytes 1769476
  93.8 0.8 copy-start.10
  93.8 1.4 %copy-start.4 = (f32[3,128,128]{2,1,0:T(8,128)S(1)}, f32[3,128,128]{2,1,0:T(8,128)}, u32[]{:S(2)}) copy-start(f32[3,128,128]{2,1,0:T(8,128)} %get-tuple-element.30) | copy-start | bytes 589828
  94.6 2.5 %copy-start.1 = (f32[3,256,128]{2,1,0:T(8,128)S(1)}, f32[3,256,128]{2,1,0:T(8,128)}, u32[]{:S(2)}) copy-start(f32[3,256,128]{2,1,0:T(8,128)} %get-tuple-element.33) | copy-start | bytes 1179652
  95.2 0.7 copy-start.9
  95.9 0.7 copy-start.8
  97.2 0.8 copy-start.7
  97.2 1.3 %copy-start.3 = (f32[3,128,128]{2,1,0:T(8,128)S(1)}, f32[3,128,128]{2,1,0:T(8,128)}, u32[]{:S(2)}) copy-start(f32[3,128,128]{2,1,0:T(8,128)} %get-tuple-element.35) | copy-start | bytes 589828
  98.5 0.7 copy-start.6
  98.5 1.9 %copy-start.2 = (f32[3,128,128]{2,1,0:T(8,128)S(1)}, f32[3,128,128]{2,1,0:T(8,128)}, u32[]{:S(2)}) copy-start(f32[3,128,128]{2,1,0:T(8,128)} %get-tuple-element.38) | copy-start | bytes 589828
  99.2 0.7 copy-start.5

commit v2 on v1

--- a/solution.py
+++ b/solution.py
@@ -10,6 +10,7 @@
 F32 = jnp.float32
 BF16 = jnp.bfloat16
 EPS = 1e-05
+G_local, G_edge, G_edge_back, G_grads = 1, 2, 2, 1
 
 
 def mm(a, b):
@@ -51,6 +52,15 @@
     return jnp.sum(jnp.where(eye, row.astype(F32), 0.0), axis=1, keepdims=True)
 
 
+def grouped(tiles, group, body):
+    def several(t, carry):
+        for i in range(group):
+            body(t * group + i)
+        return carry
+
+    lax.fori_loop(0, tiles // group, several, 0)
+
+
 def silu_parts(x):
     sig = 0.5 * jnp.tanh(0.5 * x) + 0.5
     return x * sig, sig * (1.0 + x * (1.0 - sig))
@@ -60,7 +70,7 @@
     nd, ns, layers, n, e, sr, D, te, r2 = dims
     (nodes, edges, snd, rcv, live, flags, send,
      w1, b1, w2, o1, g1, wn, nb, wn2, no, ng, wo, gout,
-     out_l, out_g, q_w1, q_b1, q_w2, q_o1, q_g1, q_wn, q_nb, q_wn2, q_no, q_ng, q_wo,
+     out_l, out_g, out_q, out_b,
      ohs, ohst, ohr, ohrt, ohx, ohxt, fcol,
      c_w1, c_w2, c_wn, c_wn2, c_wo,
      joined, act, ds1, xhat, rstd, estate, summed,
@@ -128,17 +138,23 @@
 
     def build(ids, count, oh, oht, mask):
         width = oh.shape[1]
+        short = jnp.int16
+        down = lax.broadcasted_iota(jnp.int32, (width, 128), 0).astype(short)
+        across = lax.broadcasted_iota(jnp.int32, (16, width), 1).astype(short)
+        across = jnp.concatenate([across] * 8, axis=0)
+
+        def hit(a, b):
+            return jnp.where(a == b, jnp.ones(a.shape, BF16), jnp.zeros(a.shape, BF16))
 
         def body(r, carry):
             row = ids[pl.ds(r, 1), :]
             if mask is not None:
                 row = jnp.where(mask[pl.ds(r, 1), :] > 0, row, -1)
             at = pl.multiple_of(r * 128, 128)
-            down = lax.broadcasted_iota(jnp.int32, (width, 128), 0)
-            oht[:, pl.ds(at, 128)] = jnp.where(down == row, 1.0, 0.0).astype(BF16)
-            col = as_column(row).astype(jnp.int32)
-            across = lax.broadcasted_iota(jnp.int32, (128, width), 1)
-            oh[pl.ds(at, 128), :] = jnp.where(across == col, 1.0, 0.0).astype(BF16)
+            wide = jnp.broadcast_to(row, (16, 128)).astype(short)
+            oht[:, pl.ds(at, 128)] = hit(down, jnp.concatenate([wide] * (width // 16), axis=0))
+            col = jnp.broadcast_to(as_column(row).astype(jnp.int32), (128, 128)).astype(short)
+            oh[pl.ds(at, 128), :] = hit(across, jnp.concatenate([col] * (width // 128), axis=1))
             return carry
 
         lax.fori_loop(0, count // 128, body, 0)
@@ -179,19 +195,18 @@
     for layer in range(layers):
         own = nin[layer, :, 0:D]
 
-        def local(t, carry, layer=layer):
+        def local(t, layer=layer):
             rows = pl.ds(pl.multiple_of(t * te, te), te)
             own = nin[layer, :, 0:D]
             joined[layer, rows, 0:D] = estate[rows, :].astype(BF16)
             joined[layer, rows, D:2 * D] = mm(ohs[rows, 0:n], own).astype(BF16)
             joined[layer, rows, 2 * D:3 * D] = mm(ohr[rows, :], own).astype(BF16)
-            return carry
-
-        lax.fori_loop(0, tiles, local, 0)
+
+        grouped(tiles, G_local, local)
         summed[...] = jnp.zeros_like(summed)
         wait_moves(halo_copy, layer, has_next, has_prev)
 
-        def edge(t, carry, layer=layer):
+        def edge(t, layer=layer):
             rows = pl.ds(pl.multiple_of(t * te, te), te)
             far = mm(ohs[rows, n:], halo[layer])
             xs = (joined[layer, rows, D:2 * D].astype(F32) + far).astype(BF16)
@@ -210,9 +225,8 @@
             msg = g1[pl.ds(layer, 1), :] * xh
             estate[rows, :] += msg
             summed[...] += mm(ohrt[:, rows], msg.astype(BF16))
-            return carry
-
-        lax.fori_loop(0, tiles, edge, 0)
+
+        grouped(tiles, G_edge, edge)
 
         sh = summed[...].astype(BF16)
         nin[layer, :, D:2 * D] = sh
@@ -296,10 +310,7 @@
 
     def stage5(layer):
         wait_all(s4, layer, ns)
-        at = 0
-        for out, count in ((q_w1, k1), (q_w2, hid_rows), (q_wn, kn), (q_wn2, D), (q_wo, D)):
-            out[layer] = g4[layer, pl.ds(at, count), :].astype(F32)
-            at += count
+        out_q[layer] = g4[layer]
 
     def norm_back(dxh, xh, rs):
         return rs * (dxh - lmean(dxh) - xh * lmean(dxh * xh))
@@ -325,7 +336,7 @@
         dext[...] = jnp.zeros_like(dext)
         glat[...] = g + dnin[:, :D]
 
-        def edge_back(t, carry, layer=layer, row=row):
+        def edge_back(t, layer=layer, row=row):
             rows = pl.ds(pl.multiple_of(t * te, te), te)
             dmsg = dedge[rows, :] + mm(ohr[rows, :], dsh[...])
             xh = xhat[layer, rows, :]
@@ -344,22 +355,20 @@
             glat[...] += mm(ohrt[:, rows], dj[:, 2 * D:])
             if layer > 0:
                 dedge[rows, :] += dj[:, 0:D].astype(F32)
-            return carry
-
-        lax.fori_loop(0, tiles, edge_back, 0)
+
+        grouped(tiles, G_edge_back, edge_back)
         hgrad[layer] = dext[n:, :].astype(BF16)
         start_moves(back_copy, layer, has_prev)
 
         acc1[...] = jnp.zeros_like(acc1)
         acc2[...] = jnp.zeros_like(acc2)
 
-        def grads(t, carry, layer=layer):
+        def grads(t, layer=layer):
             rows = pl.ds(pl.multiple_of(t * te, te), te)
             acc1[...] += mm_tn(joined[layer, rows, :], dp1[rows, :])
             acc2[...] += mm_tn(act[layer, rows, :], dp2[rows, :])
-            return carry
-
-        lax.fori_loop(0, tiles, grads, 0)
+
+        grouped(tiles, G_grads, grads)
         at = 0
         for value in (acc1[...], acc2[...], mm_tn(nin[layer], dpre),
                       mm_tn(hid[layer], dtwo), mm_tn(nin[layer, :, D:2 * D], dout)):
@@ -398,13 +407,26 @@
     total = br2[0]
     for j in range(1, nd):
         total = total + br2[j]
-    for layer in range(layers):
-        for i, out in enumerate((q_b1, q_o1, q_g1, q_nb, q_no, q_ng)):
-            out[pl.ds(layer, 1), :] = total[layer * 6 + i:layer * 6 + i + 1, :]
+    out_b[...] = total
     stage4(0)
     if layers > 1:
         stage5(1)
     stage5(0)
+
+
+def finish(layers, lat, glat, grads, sums, out_l, out_g, *outs):
+    q_w1, q_b1, q_w2, q_o1, q_g1, q_wn, q_nb, q_wn2, q_no, q_ng, q_wo = outs
+    out_l[...] = lat[...]
+    out_g[...] = glat[...]
+    at = 0
+    for out in (q_w1, q_w2, q_wn, q_wn2, q_wo):
+        count = out.shape[1]
+        for layer in range(layers):
+            out[layer] = grads[layer, pl.ds(at, count), :].astype(F32)
+        at += count
+    for layer in range(layers):
+        for i, out in enumerate((q_b1, q_o1, q_g1, q_nb, q_no, q_ng)):
+            out[pl.ds(layer, 1), :] = sums[pl.ds(layer * 6 + i, 1), :]
 
 
 def on_device(nd, ns, nodes, edges, senders, receivers, edge_live, outlet_flags, send_rows, *rest):
@@ -413,7 +435,7 @@
     e = edges.shape[0]
     sr = send_rows.shape[0]
     layers = weights[0].shape[0]
-    te = min(512, e)
+    te = min(1024, e)
     grad_rows = sum(w.shape[1] for w in weights if w.ndim == 3)
     r2 = pl.cdiv(grad_rows, ns * nd * 16) * 16
     c1 = nd * r2
@@ -450,16 +472,26 @@
     rows = lambda v: v.reshape(-1, 128)
     args = (nodes, edges, rows(senders), rows(receivers), rows(edge_live), rows(outlet_flags),
             rows(send_rows), *weights, grad_out)
-    return tuple(pl.pallas_call(
+    mid = shapes[:2] + [
+        jax.ShapeDtypeStruct((layers, total, D), BF16),
+        jax.ShapeDtypeStruct((brows, D), F32),
+    ]
+    found = pl.pallas_call(
         functools.partial(kernel, dims),
-        out_shape=shapes,
+        out_shape=mid,
         in_specs=[vmem] * len(args),
-        out_specs=[vmem] * len(shapes),
+        out_specs=[vmem] * len(mid),
         scratch_shapes=scratch,
         compiler_params=pltpu.CompilerParams(
             collective_id=0, has_side_effects=True, vmem_limit_bytes=60 * 1024 * 1024
         ),
-    )(*args))
+    )(*args)
+    return tuple(pl.pallas_call(
+        functools.partial(finish, layers),
+        out_shape=shapes,
+        in_specs=[vmem] * len(mid),
+        out_specs=[vmem] * len(shapes),
+    )(*found))
 
 
 def solution(mesh):

time: 101 us -> 80 us (0.79)
  local copies, waits for them, and re-layouts: 10.7 us -> 0 us
  Pallas kernels: 89.7 us -> 79.1 us
    unnamed x35 -> x0, local copies, waits for them, and re-layouts: 10.7 us -> none
    pallas_call x1 -> x2, Pallas kernels: 89.7 us -> 79.1 us  [the longest x1 76.5 us: on_device(): pl.pallas_call(functools.partial(kernel, dims), out_shape=mid, in_specs=[...]
where the time goes in v2:
time: 80 us; the launch traced here: 79.9 us
  Pallas kernels  79.1 us (99%)
    pallas_call x1, Pallas kernels, on_device(): pl.pallas_call(functools.partial(kernel, dims), out_shape=mid, in_specs=[...  76.5 us
    pallas_call x1, Pallas kernels, on_device(): pl.pallas_call(functools.partial(finish, layers), out_shape=shapes, in_sp...  2.64 us

profile of v2, /device:TPU:1, one launch (start us, length us, event | category | flops | bytes accessed | tf_op | source)
XLA Modules:
  0.0 79.9 jit_solution(17442379034022451489)
XLA Ops:
  0.7 76.5 %shard_map.282 = (f32[512,128]{1,0:T(8,128)}, f32[512,128]{1,0:T(8,128)}, bf16[3,1024,128]{2,1,0:T(8,128)(2,1)}, f32[24,128]{1,0:T(8,128)}) custom-call(bf16[512,128]{1,0:T(8,128)(2,1)} %refs_0_.1, bf16[2048,128]{1,0:T(8,128)(2,1)} %refs_1_.1, s32[16,128]{1,0:T(8,128)} %bitcast.5, s32[16,128]{1,0:T(8,128)} %bitcast.6, s32[16,128]{1,0:T(8,128)} %bitcast.7, ...), custom_call_target="tpu_custom_call" | custom-call | tf_op jit(solution)/shard_map/pallas_call | solution.py:479
  77.1 2.6 %shard_map.283 = (f32[512,128]{1,0:T(8,128)}, f32[512,128]{1,0:T(8,128)}, f32[3,384,128]{2,1,0:T(8,128)}, f32[3,128]{1,0:T(4,128)}, f32[3,128,128]{2,1,0:T(8,128...) custom-call(f32[512,128]{1,0:T(8,128)} %get-tuple-element.17.lat, ...), custom_call_target="tpu_custom_call" | custom-call | tf_op jit(solution)/shard_map/pallas_call | solution.py:489

commit v3 on v2

--- a/solution.py
+++ b/solution.py
@@ -10,7 +10,7 @@
 F32 = jnp.float32
 BF16 = jnp.bfloat16
 EPS = 1e-05
-G_local, G_edge, G_edge_back, G_grads = 1, 2, 2, 1
+G_local, G_edge, G_edge_back, G_grads = 2, 2, 2, 2
 
 
 def mm(a, b):
@@ -350,11 +350,11 @@
             bacc[pl.ds(row, 1), :] += rsum(dpre)
             dpre = dpre.astype(BF16)
             dp1[rows, :] = dpre
-            dj = mm_nt(dpre, c_w1[layer]).astype(BF16)
-            dext[...] += mm(ohst[:, rows], dj[:, D:2 * D])
-            glat[...] += mm(ohrt[:, rows], dj[:, 2 * D:])
+            dj = mm_nt(dpre, c_w1[layer, D:3 * D, :]).astype(BF16)
+            dext[...] += mm(ohst[:, rows], dj[:, 0:D])
+            glat[...] += mm(ohrt[:, rows], dj[:, D:2 * D])
             if layer > 0:
-                dedge[rows, :] += dj[:, 0:D].astype(F32)
+                dedge[rows, :] += mm_nt(dpre, c_w1[layer, 0:D, :]).astype(BF16).astype(F32)
 
         grouped(tiles, G_edge_back, edge_back)
         hgrad[layer] = dext[n:, :].astype(BF16)

time: 80 us -> 78.7 us (0.984)
  Pallas kernels: 79.1 us -> 77.8 us
    pallas_call x1, Pallas kernels: 76.5 us -> 75.2 us  [on_device(): pl.pallas_call(functools.partial(kernel, dims), out_shape=mid, in_specs=[...]
where the time goes in v3:
time: 78.7 us; the launch traced here: 78.6 us
  Pallas kernels  77.8 us (99%)
    pallas_call x1, Pallas kernels, on_device(): pl.pallas_call(functools.partial(kernel, dims), out_shape=mid, in_specs=[...  75.2 us
    pallas_call x1, Pallas kernels, on_device(): pl.pallas_call(functools.partial(finish, layers), out_shape=shapes, in_sp...  2.64 us

profile of v3, /device:TPU:1, one launch (start us, length us, event | category | flops | bytes accessed | tf_op | source)
XLA Modules:
  0.0 78.6 jit_solution(12276744006230111034)
XLA Ops:
  0.7 75.2 %shard_map.282 = (f32[512,128]{1,0:T(8,128)}, f32[512,128]{1,0:T(8,128)}, bf16[3,1024,128]{2,1,0:T(8,128)(2,1)}, f32[24,128]{1,0:T(8,128)}) custom-call(bf16[512,128]{1,0:T(8,128)(2,1)} %refs_0_.1, bf16[2048,128]{1,0:T(8,128)(2,1)} %refs_1_.1, s32[16,128]{1,0:T(8,128)} %bitcast.5, s32[16,128]{1,0:T(8,128)} %bitcast.6, s32[16,128]{1,0:T(8,128)} %bitcast.7, ...), custom_call_target="tpu_custom_call" | custom-call | tf_op jit(solution)/shard_map/pallas_call | solution.py:479
  75.8 2.6 %shard_map.283 = (f32[512,128]{1,0:T(8,128)}, f32[512,128]{1,0:T(8,128)}, f32[3,384,128]{2,1,0:T(8,128)}, f32[3,128]{1,0:T(4,128)}, f32[3,128,128]{2,1,0:T(8,128...) custom-call(f32[512,128]{1,0:T(8,128)} %get-tuple-element.17.lat, ...), custom_call_target="tpu_custom_call" | custom-call | tf_op jit(solution)/shard_map/pallas_call | solution.py:489
